TPU v7x, 32 devices: a whole 2x2x4 slice. The times are simulated.
32 devices in a mesh: inst: 2 (over core), lon: 16 (over z, y, x).
Axes of the slice: x: 2, y: 2, z: 4, core: 2. Of those that a mesh axis runs over, the one named last changes fastest.
Arguments:
- obs_x: bfloat16 [384, 128, 256], P(('inst', 'lon')), may hold values from -6 to 6
- obs_cot: bfloat16 [384, 128, 256], P(('inst', 'lon')), may hold values from -6 to 6
- tile_window: int32 [384, 2], P(('inst', 'lon')), may hold values from 0 to 179, as said below
- point_mask: int32 [384, 128], P(('inst', 'lon')), may hold values from 0 to 1, as said below
- band_counts: int32 [32], P(('inst', 'lon')), may hold values from 1 to 12, as said below
- latents: bfloat16 [64, 184, 256], P('lon'), may hold values from -6 to 6
- w_query: bfloat16 [256, 128], replicated, may hold values from -3 to 3
- w_key: bfloat16 [256, 128], replicated, may hold values from -0.375 to 0.375
- w_value: bfloat16 [256, 128], replicated, may hold values from -0.375 to 0.375
- w_out: bfloat16 [128, 256], replicated, may hold values from -0.5 to 0.5
Outputs:
- decoded: bfloat16 [384, 128, 256], P(('inst', 'lon'))
- obs_grad: bfloat16 [384, 128, 256], P(('inst', 'lon'))
- latent_grad: float32 [64, 184, 256], P('lon')
- query_grad: float32 [256, 128], replicated
- key_grad: float32 [256, 128], replicated
- value_grad: float32 [256, 128], replicated
- out_grad: float32 [128, 256], replicated
Inputs may be any that keep to these rules, and one draw needn't show every extreme that they name: `tile_window`: column 0 is the first longitude column of the tile's window; the window's centre column (column 2) mod 64 is one of the 4 columns of the band that holds the tile. Column 1 is the window's first latitude row, at most 179. `point_mask`: in each tile the live slots come first, and half or more of the slots are live. `band_counts`: one entry equals 12.
All inputs are finite; a program needn't handle non-finite values.
Results may differ from a plain program's by a relative error of at most 0.007.
The roundings to bfloat16 on the way count: a program that leaves them out, or rounds other values in their place, can miss the bound.
Values may be sent and summed in bfloat16 or wider, within the bound.
A program may use at most 64 MiB of HBM per device.

v0:
```python
import math
import jax
import jax.numpy as jnp
from jax import lax
from jax.sharding import PartitionSpec as P

HEADS = 4
REACH = 2
softcap = 30.0


def with_halo(block, sides, width):
    for axis, dim in sides:
        count = lax.axis_size(axis)
        forward = [(i, i + 1) for i in range(count - 1)]
        forward.append((count - 1, 0))
        backward = [(target, source) for source, target in forward]
        low = lax.ppermute(
            lax.slice_in_dim(block, block.shape[dim] - width, None, axis=dim), axis, forward
        )
        high = lax.ppermute(lax.slice_in_dim(block, 0, width, axis=dim), axis, backward)
        block = jnp.concatenate([low, block, high], axis=dim)
    return block


def passed_along(block, axis, distance):
    devices = range(lax.axis_size(axis))
    route = [((i - distance) % len(devices), i) for i in devices]
    return lax.ppermute(block, axis, route)


def split_products(grad, w_pair, flat_latents):
    grad_high = grad.astype(jnp.bfloat16)
    grad_low = (grad - grad_high.astype(jnp.float32)).astype(jnp.bfloat16)
    by_rows = (((1,), (1,)), ((), ()))
    by_cols = (((0,), (0,)), ((), ()))
    latent_part = lax.dot_general(
        grad_high, w_pair, by_rows, preferred_element_type=jnp.float32
    ) + lax.dot_general(grad_low, w_pair, by_rows, preferred_element_type=jnp.float32)
    pair_weight = lax.dot_general(
        flat_latents, grad_high, by_cols, preferred_element_type=jnp.float32
    ) + lax.dot_general(flat_latents, grad_low, by_cols, preferred_element_type=jnp.float32)
    return (latent_part, pair_weight)


def attend(obs_x, obs_cot, live_points, windows, w_query, w_out):
    n_tiles, tile_len, model_width = obs_x.shape
    attn_width = w_query.shape[1]
    head_size = attn_width // HEADS
    score_scale = 1.0 / math.sqrt(head_size)
    flat_x = obs_x.reshape(-1, model_width)
    queries = jnp.dot(flat_x, w_query, preferred_element_type=jnp.float32).astype(jnp.bfloat16)
    query_heads = queries.reshape(n_tiles, tile_len, HEADS, head_size)
    win_keys = windows[:, :, :attn_width].reshape(n_tiles, -1, HEADS, head_size)
    win_values = windows[:, :, attn_width:].reshape(n_tiles, -1, HEADS, head_size)
    raw_scores = (
        jnp.einsum("nqhd,nkhd->nhqk", query_heads, win_keys, preferred_element_type=jnp.float32)
        * score_scale
    )
    capped = softcap * jnp.tanh(raw_scores / softcap)
    weights = jnp.exp(capped)
    probs = weights / jnp.sum(weights, axis=-1, keepdims=True)
    probs_b = probs.astype(jnp.bfloat16)
    attended = jnp.einsum(
        "nhqk,nkhd->nqhd", probs_b, win_values, preferred_element_type=jnp.float32
    )
    attended = attended.astype(jnp.bfloat16).reshape(-1, attn_width)
    projected = jnp.dot(attended, w_out, preferred_element_type=jnp.float32).reshape(
        n_tiles, tile_len, model_width
    )
    decoded = (obs_x.astype(jnp.float32) + live_points[:, :, None] * projected).astype(jnp.bfloat16)
    masked = obs_cot * live_points.astype(jnp.bfloat16)[:, :, None]
    flat_cot = masked.reshape(-1, model_width)
    out_grad = jnp.dot(attended.T, flat_cot, preferred_element_type=jnp.float32)
    attended_grad = jnp.dot(flat_cot, w_out.T, preferred_element_type=jnp.float32).astype(
        jnp.bfloat16
    )
    attended_grad = attended_grad.reshape(n_tiles, tile_len, HEADS, head_size)
    prob_grad = jnp.einsum(
        "nqhd,nkhd->nhqk", attended_grad, win_values, preferred_element_type=jnp.float32
    )
    row_inner = jnp.sum(probs * prob_grad, axis=-1, keepdims=True)
    score_grad = (
        probs * (prob_grad - row_inner) * (1.0 - (capped / softcap) ** 2) * score_scale
    ).astype(jnp.bfloat16)
    query_part = jnp.einsum(
        "nhqk,nkhd->nqhd", score_grad, win_keys, preferred_element_type=jnp.float32
    )
    query_part = query_part.astype(jnp.bfloat16).reshape(-1, attn_width)
    key_part = jnp.einsum(
        "nhqk,nqhd->nkhd", score_grad, query_heads, preferred_element_type=jnp.float32
    )
    value_part = jnp.einsum(
        "nhqk,nqhd->nkhd", probs_b, attended_grad, preferred_element_type=jnp.float32
    )
    window_grad = jnp.concatenate(
        [key_part.reshape(n_tiles, -1, attn_width), value_part.reshape(n_tiles, -1, attn_width)],
        axis=-1,
    )
    obs_grad = obs_cot.astype(jnp.float32).reshape(-1, model_width) + jnp.dot(
        query_part, w_query.T, preferred_element_type=jnp.float32
    )
    obs_grad = obs_grad.astype(jnp.bfloat16).reshape(n_tiles, tile_len, model_width)
    query_grad = jnp.dot(flat_x.T, query_part, preferred_element_type=jnp.float32)
    return (decoded, obs_grad, window_grad, query_grad, out_grad)


def shards(
    obs_x, obs_cot, tile_window, point_mask, band_counts, latents, w_query, w_key, w_value, w_out
):
    band_cols, lat_rows, model_width = latents.shape
    attn_width = w_query.shape[1]
    lon_cols = band_cols * lax.axis_size("lon")
    window = 2 * REACH + 1
    w_pair = jnp.concatenate([w_key, w_value], axis=1)
    own_pairs = jnp.dot(
        latents.reshape(-1, model_width), w_pair, preferred_element_type=jnp.float32
    ).astype(jnp.bfloat16)
    own_pairs = own_pairs.reshape(band_cols, lat_rows, 2 * attn_width)
    wide_pairs = with_halo(own_pairs, (("lon", 0),), REACH).reshape(-1, 2 * attn_width)
    band_first = lax.axis_index("lon") * band_cols
    offsets = jnp.arange(window, dtype=jnp.int32)
    starts = (tile_window[:, 0:1] - band_first + REACH) % lon_cols + offsets[None, :]
    lat_index = tile_window[:, 1:2] + offsets[None, :]
    key_index = (starts[:, :, None] * lat_rows + lat_index[:, None, :]).reshape(-1, window * window)
    windows = jnp.take(wide_pairs, key_index, axis=0)
    local_tile = jnp.arange(obs_x.shape[0], dtype=jnp.int32)
    live_points = (
        point_mask.astype(jnp.float32) * (local_tile < band_counts[0]).astype(jnp.float32)[:, None]
    )
    decoded, obs_grad, window_grad, query_grad, out_grad = attend(
        obs_x, obs_cot, live_points, windows, w_query, w_out
    )
    wide_cols = band_cols + 2 * REACH
    pair_grad = jnp.zeros((wide_cols * lat_rows, 2 * attn_width), jnp.float32)
    pair_grad = pair_grad.at[key_index.reshape(-1)].add(window_grad.reshape(-1, 2 * attn_width))
    pair_grad = pair_grad.reshape(wide_cols, lat_rows, 2 * attn_width)
    from_right = passed_along(pair_grad[:REACH].astype(jnp.bfloat16), "lon", -1).astype(jnp.float32)
    from_left = passed_along(pair_grad[band_cols + REACH :].astype(jnp.bfloat16), "lon", 1).astype(
        jnp.float32
    )
    own_grad = pair_grad[REACH : band_cols + REACH]
    own_grad = own_grad.at[:REACH].add(from_left)
    own_grad = own_grad.at[band_cols - REACH :].add(from_right)
    flat_grad = own_grad.reshape(-1, 2 * attn_width)
    flat_latents = latents.reshape(-1, model_width)
    latent_part, pair_weight = split_products(flat_grad, w_pair, flat_latents)
    latent_grad = lax.psum(latent_part, "inst")
    query_grad, out_grad, pair_weight = lax.psum(
        (query_grad, out_grad, pair_weight), ("inst", "lon")
    )
    return (
        decoded,
        obs_grad,
        latent_grad.reshape(band_cols, lat_rows, model_width),
        query_grad,
        pair_weight[:, :attn_width],
        pair_weight[:, attn_width:],
        out_grad,
    )


def solution(mesh):
    placed = (
        P(("inst", "lon"), None, None),
        P(("inst", "lon"), None, None),
        P(("inst", "lon"), None),
        P(("inst", "lon"), None),
        P(("inst", "lon")),
        P("lon", None, None),
        P(),
        P(),
        P(),
        P(),
    )
    return jax.shard_map(
        shards,
        mesh=mesh,
        in_specs=placed,
        out_specs=(
            P(("inst", "lon"), None, None),
            P(("inst", "lon"), None, None),
            P("lon", None, None),
            P(),
            P(),
            P(),
            P(),
        ),
        check_vma=False,
    )
```

profile of v0, /device:TPU:0, one launch (start us, length us, event | category | flops | bytes accessed | tf_op | source)
XLA Modules:
  0.0 227.1 jit_solution(15239581388625097601)
XLA Ops:
  10.1 7.0 %collective-permute-start.1 = (bf16[2,184,256]{2,1,0:T(8,128)(2,1)}, bf16[2,184,256]{2,1,0:T(8,128)(2,1)}, u32[]{:S(2)}, u32[]{:S(2)}) collective-permute-start(bf16[2,184,256]{2,1,0:T(8,128)(2,1)} %bitcast.7), channel_id=1, source_target_pairs={{1,0},{2,1},{3,2},{4,3},{5,4},{6,5},{7,6},{8,7},{9,8},{10,9},{11,1... | collective-permute-start | bytes 565256 | tf_op jit(solution)/shard_map/ppermute | solution.py:21
  19.3 1.1 reshape.270
  21.1 1.4 broadcast_multiply_fusion
  22.5 1.1 convolution_convert_fusion
  23.6 1.2 copy.37
  24.7 1.1 reshape.275
  27.2 1.1 pad_maximum_fusion
  28.3 2.0 gather_fusion
  31.8 1.2 fusion.36
  34.3 1.1 convolution_convert_fusion.3
  35.4 3.2 %fusion.8 = bf16[12,128,4,32]{1,3,2,0:T(8,128)(2,1)} fusion(bf16[12,25,4,32]{1,3,2,0:T(8,128)(2,1)S(1)} %bitcast.118, f32[12,4,128,25]{2,3,1,0:T(8,128)} %fusion.36, f32[12,4,128,25]{2,3,1,0:T(8,128)} %copy-done.23, f32[12,4,128]{2,1,0:T(4,128)S(1)} %get-tuple-element.62), kind=kOutput, calls=%fused_computation.21 | convolution fusion | flops 11876376 | bytes 1723392 | tf_op jit(solution)/shard_map/nhqk,nkhd->nqhd/dot_general | solution.py:86
  38.6 2.7 %convolution_bitcast_fusion.1 = f32[12,25,4,32]{1,3,2,0:T(8,128)S(1)} fusion(f32[12,4,128,25]{2,3,1,0:T(8,128)} %fusion.36, f32[12,4,128,25]{2,3,1,0:T(8,128)} %copy-done.23, bf16[12,128,4,32]{1,0,3,2:T(8,128)(2,1)} %reshape.270, f32[12,4,128]{2,1,0:T(4,128)S(1)} %get-tuple-element.62), kind=kOutput, calls=%fused_computation.12 | convolution fusion | flops 11679768 | bytes 1800192 | tf_op jit(solution)/shard_map/nhqk,nqhd->nkhd/dot_general | solution.py:90
  41.3 2.4 %convolution_bitcast_fusion = f32[12,25,4,32]{1,3,2,0:T(8,128)} fusion(bf16[12,128,4,32]{1,0,3,2:T(8,128)(2,1)S(1)} %copy-done.6, f32[12,4,128,25]{2,3,1,0:T(8,128)} %copy-done.23, f32[12,4,128]{2,1,0:T(4,128)S(1)} %get-tuple-element.62), kind=kOutput, calls=%fused_computation.11 | convolution fusion | flops 10291200 | bytes 1185792 | tf_op jit(solution)/shard_map/nhqk,nqhd->nkhd/dot_general | solution.py:93
  43.6 1.5 copy.45
  47.4 3.0 %scatter_custom_fusion = f32[1472,256]{1,0:T(8,128)S(1)} fusion(s32[300]{0:T(512)} %fusion.45, f32[]{:T(128)} %constant.106.clone.1, f32[300,128]{1,0:T(8,128)} %concatenate.21, f32[]{:T(128)} %constant.116, f32[300,128]{1,0:T(8,128)} %concatenate.20), kind=kCustom, calls=%fused_computation.37 | custom fusion | flops 153600 | bytes 1819648 | tf_op jit(solution)/shard_map/scatter-add | solution.py:136
  53.3 5.6 %collective-permute-start.3 = (bf16[2,184,256]{2,1,0:T(8,128)(2,1)S(1)}, bf16[2,184,256]{2,1,0:T(8,128)(2,1)S(1)}, u32[]{:S(2)}, u32[]{:S(2)}) collective-permute-start(bf16[2,184,256]{2,1,0:T(8,128)(2,1)S(1)} %bitcast.119), channel_id=1, source_target_pairs={{1,0},{2,1},{3,2},{4,3},{5,4},{6,5},{7,6},{8,7},{9,8},{10,9},{11,1... | collective-permute-start | bytes 565256 | tf_op jit(solution)/shard_map/ppermute | solution.py:29
  59.9 2.6 %collective-permute-done.2 = bf16[2,184,256]{2,1,0:T(8,128)(2,1)S(1)} collective-permute-done((bf16[2,184,256]{2,1,0:T(8,128)(2,1)S(1)}, bf16[2,184,256]{2,1,0:T(8,128)(2,1)S(1)}, u32[]{:S(2)}, u32[]{:S(2)}) %collective-permute-start.2) | collective-permute-done | bytes 188448 | tf_op jit(solution)/shard_map/ppermute | solution.py:29
  65.2 2.2 convolution_add_fusion.1
  67.5 1.3 fusion.1
  68.8 1.3 add_convert_fusion
  70.1 126.6 %all-reduce.6.cloned.1.call-done = (f32[256,128]{0,1:T(8,128)}, f32[256,256]{0,1:T(8,128)}, f32[128,256]{1,0:T(8,128)}) async-done(((f32[256,128]{0,1:T(8,128)}, f32[256,256]{0,1:T(8,128)}, f32[128,256]{1,0:T(8,128)}), (f32[256,128]{0,1:T(8,128)}, f32[256,256]{0,1:T(8,128)}, f32[128,256]{1,0:T(8,128)})) %all-reduce.6.cloned.1.call-update) | async-done | bytes 524304 | tf_op jit(solution)/shard_map/psum | solution.py:149
  196.7 1.7 copy.47
  200.9 16.7 %all-reduce.4.cloned.1.call-done = f32[4,184,256]{2,1,0:T(8,128)} async-done(((f32[4,184,256]{2,1,0:T(8,128)}), f32[4,184,256]{2,1,0:T(8,128)}) %all-reduce.4.cloned.1.call-update) | async-done | bytes 753680 | tf_op jit(solution)/shard_map/psum | solution.py:148
  217.6 2.0 copy.87
  (109 shorter events, 21.0 us)
Async XLA Ops:
  7.2 1.9 copy-start
  7.2 9.9 %copy-start.22 = (s32[12,2]{0,1:T(2,128)S(1)}, s32[12,2]{0,1:T(2,128)}, u32[]{:S(2)}) copy-start(s32[12,2]{0,1:T(2,128)} %param.16) | copy-start | bytes 292
  7.2 11.5 %copy-start.15 = (bf16[256,128]{1,0:T(8,128)(2,1)S(1)}, bf16[256,128]{1,0:T(8,128)(2,1)}, u32[]{:S(2)}) copy-start(bf16[256,128]{1,0:T(8,128)(2,1)} %param.20) | copy-start | bytes 196612
  7.2 11.5 %copy-start.2 = (bf16[12,128,256]{2,1,0:T(8,128)(2,1)S(1)}, bf16[12,128,256]{2,1,0:T(8,128)(2,1)}, u32[]{:S(2)}) copy-start(bf16[12,128,256]{2,1,0:T(8,128)(2,1)} %param.14) | copy-start | bytes 2359300
  7.2 189.5 %all-reduce.6.cloned.1.call-start = ((), (), s32[]{:S(2)}) async-start(), calls=%async_computation.1 | async-start | bytes 1048576 | tf_op jit(solution)/shard_map/psum | solution.py:149
  9.1 10.0 %copy-start.7 = (bf16[256,256]{1,0:T(8,128)(2,1)}, bf16[256,256]{1,0:T(8,128)(2,1)S(1)}, u32[]{:S(2)}) copy-start(bf16[256,256]{1,0:T(8,128)(2,1)S(1)} %constant_dynamic-update-slice_fusion) | copy-start | bytes 393220
  10.1 16.3 %collective-permute-start.1 = (bf16[2,184,256]{2,1,0:T(8,128)(2,1)}, bf16[2,184,256]{2,1,0:T(8,128)(2,1)}, u32[]{:S(2)}, u32[]{:S(2)}) collective-permute-start(bf16[2,184,256]{2,1,0:T(8,128)(2,1)} %bitcast.7), channel_id=1, source_target_pairs={{1,0},{2,1},{3,2},{4,3},{5,4},{6,5},{7,6},{8,7},{9,8},{10,9},{11,1... | collective-permute-start | bytes 565256 | tf_op jit(solution)/shard_map/ppermute | solution.py:21
  17.1 10.1 %collective-permute-start = (bf16[2,184,256]{2,1,0:T(8,128)(2,1)}, bf16[2,184,256]{2,1,0:T(8,128)(2,1)}, u32[]{:S(2)}, u32[]{:S(2)}) collective-permute-start(bf16[2,184,256]{2,1,0:T(8,128)(2,1)} %bitcast.5), channel_id=1, source_target_pairs={{0,1},{1,2},{2,3},{3,4},{4,5},{5,6},{6,7},{7,8},{8,9},{9,10},{10,1... | collective-permute-start | bytes 565256 | tf_op jit(solution)/shard_map/ppermute | solution.py:18
  18.5 1.9 copy-start.21
  19.1 3.4 %copy-start.17 = (bf16[128,256]{1,0:T(8,128)(2,1)S(1)}, bf16[128,256]{1,0:T(8,128)(2,1)}, u32[]{:S(2)}) copy-start(bf16[128,256]{1,0:T(8,128)(2,1)} %param.23) | copy-start | bytes 196612
  30.3 1.5 copy-start.6
  30.5 2.5 %copy-start.11 = (bf16[12,128,4,32]{1,0,3,2:T(8,128)(2,1)S(1)}, bf16[12,128,4,32]{1,0,3,2:T(8,128)(2,1)}, u32[]{:S(2)}) copy-start(bf16[12,128,4,32]{1,0,3,2:T(8,128)(2,1)} %reshape.270) | copy-start | bytes 1179652
  50.5 2.4 %copy-start.9 = (bf16[12,4,32,128]{3,2,1,0:T(8,128)(2,1)S(1)}, bf16[12,4,32,128]{3,2,1,0:T(8,128)(2,1)}, u32[]{:S(2)}) copy-start(bf16[12,4,32,128]{3,2,1,0:T(8,128)(2,1)} %convolution_convert_fusion.3) | copy-start | bytes 1179652
  52.0 7.9 %copy-start.3 = (bf16[12,128,4,32]{1,0,3,2:T(8,128)(2,1)}, bf16[12,128,4,32]{1,0,3,2:T(8,128)(2,1)S(1)}, u32[]{:S(2)}) copy-start(bf16[12,128,4,32]{1,0,3,2:T(8,128)(2,1)S(1)} %copy.41) | copy-start | bytes 1179652
  52.9 9.6 %slice-start = ((f32[1472,256]{1,0:T(8,128)}), f32[368,256]{1,0:T(8,128)S(1)}, s32[]{:S(2)}) async-start(f32[1472,256]{1,0:T(8,128)} %copy-done.1), calls=%async_computation.2 | async-start | bytes 753664 | tf_op jit(solution)/shard_map/slice.60
  52.9 9.6 %slice-start.1 = ((f32[1472,256]{1,0:T(8,128)}), f32[736,256]{1,0:T(8,128)S(1)}, s32[]{:S(2)}) async-start(f32[1472,256]{1,0:T(8,128)} %copy-done.1), calls=%async_computation.3 | async-start | bytes 1507328 | tf_op jit(solution)/shard_map/slice | solution.py:142
  53.2 9.2 %collective-permute-start.2 = (bf16[2,184,256]{2,1,0:T(8,128)(2,1)S(1)}, bf16[2,184,256]{2,1,0:T(8,128)(2,1)S(1)}, u32[]{:S(2)}, u32[]{:S(2)}) collective-permute-start(bf16[2,184,256]{2,1,0:T(8,128)(2,1)S(1)} %bitcast.120), channel_id=1, source_target_pairs={{15,0},{0,1},{1,2},{2,3},{3,4},{4,5},{5,6},{6,7},{7,8},{8,9},{9,10... | collective-permute-start | bytes 565256 | tf_op jit(solution)/shard_map/ppermute | solution.py:29
  53.3 9.2 %collective-permute-start.3 = (bf16[2,184,256]{2,1,0:T(8,128)(2,1)S(1)}, bf16[2,184,256]{2,1,0:T(8,128)(2,1)S(1)}, u32[]{:S(2)}, u32[]{:S(2)}) collective-permute-start(bf16[2,184,256]{2,1,0:T(8,128)(2,1)S(1)} %bitcast.119), channel_id=1, source_target_pairs={{1,0},{2,1},{3,2},{4,3},{5,4},{6,5},{7,6},{8,7},{9,8},{10,9},{11,1... | collective-permute-start | bytes 565256 | tf_op jit(solution)/shard_map/ppermute | solution.py:29
  62.9 1.8 copy-start.8
  65.1 2.4 %copy-start.4 = (bf16[12,128,4,32]{1,0,3,2:T(8,128)(2,1)S(1)}, bf16[12,128,4,32]{1,0,3,2:T(8,128)(2,1)}, u32[]{:S(2)}) copy-start(bf16[12,128,4,32]{1,0,3,2:T(8,128)(2,1)} %copy-done.3) | copy-start | bytes 1179652
  65.1 2.4 %copy-start.5 = (bf16[12,128,256]{2,1,0:T(8,128)(2,1)S(1)}, bf16[12,128,256]{2,1,0:T(8,128)(2,1)}, u32[]{:S(2)}) copy-start(bf16[12,128,256]{2,1,0:T(8,128)(2,1)} %param.15) | copy-start | bytes 2359300
  65.1 2.4 %copy-start.16 = (bf16[256,128]{1,0:T(8,128)(2,1)S(1)}, bf16[256,128]{1,0:T(8,128)(2,1)}, u32[]{:S(2)}) copy-start(bf16[256,128]{1,0:T(8,128)(2,1)} %param.20) | copy-start | bytes 196612
  65.1 152.5 %all-reduce.4.cloned.1.call-start = ((), (), s32[]{:S(2)}) async-start(), calls=%async_computation | async-start | bytes 1507328 | tf_op jit(solution)/shard_map/psum | solution.py:148
  196.7 23.0 %copy-start.19 = (f32[128,256]{1,0:T(8,128)S(1)}, f32[128,256]{1,0:T(8,128)}, u32[]{:S(2)}) copy-start(f32[128,256]{1,0:T(8,128)} %get-tuple-element.72) | copy-start | bytes 393220
  (8 other events, 9.6 us)
Sparse Core Ops, SparseCore 0:
  65.2 131.4 all-reduce.5
  199.6 17.9 all-reduce.3
where the time goes:
time: 228 us; the launch traced here: 227 us
  waiting for transfers between devices  147 us (64%)
  local copies, waits for them, and re-layouts  23.6 us (10%)
  matrix products  21 us (9%)
  between operations  15.1 us (7%)
  starting transfers between devices  12.7 us (6%)
  other arithmetic  8.08 us (4%)
    psum x1, waiting for transfers between devices, shards(): lax.psum((query_grad, out_grad, pair_weight), ('inst', 'lon'))  127 us
    psum x1, waiting for transfers between devices, shards(): latent_grad = lax.psum(latent_part, 'inst')  16.7 us
    unnamed x54, local copies, waits for them, and re-layouts  9 us
    ppermute x1, starting transfers between devices, with_halo(): lax.ppermute(lax.slice_in_dim(block, 0, width, axis=dim), axis, backward)  6.97 us
    ppermute x2, starting transfers between devices, passed_along(): return lax.ppermute(block, axis, route)  5.67 us
  transfers between devices with their start and end apart: 6, of which 4 were waited for; matrix products, arithmetic and copies ran while one was open for 8% of the time, Pallas kernels for 0%

commit v1 on v0

--- a/solution.py
+++ b/solution.py
@@ -145,7 +145,8 @@
     flat_grad = own_grad.reshape(-1, 2 * attn_width)
     flat_latents = latents.reshape(-1, model_width)
     latent_part, pair_weight = split_products(flat_grad, w_pair, flat_latents)
-    latent_grad = lax.psum(latent_part, "inst")
+    pieces = lax.all_gather(latent_part, "inst", axis=0, tiled=False)
+    latent_grad = pieces.sum(axis=0)
     query_grad, out_grad, pair_weight = lax.psum(
         (query_grad, out_grad, pair_weight), ("inst", "lon")
     )

time: 228 us -> 213 us (0.934)
  waiting for transfers between devices: 147 us -> 130 us
  other arithmetic: 8.08 us -> 10.5 us
    psum x1 -> x0, waiting for transfers between devices: 16.7 us -> none  [shards(): latent_grad = lax.psum(latent_part, 'inst')]
    reduce_sum x0 -> x1, other arithmetic: none -> 2.43 us  [shards(): latent_grad = pieces.sum(axis=0)]
    unnamed x54 -> x53, local copies, waits for them, and re-layouts: 9 us -> 6.93 us
  transfers between devices with their start and end apart: 6 -> 6, of which waited for: 4 -> 3; matrix products, arithmetic and copies ran while one was open for 8% -> 9% of each run, Pallas kernels for 0% -> 0%
where the time goes in v1:
time: 213 us; the launch traced here: 212 us
  waiting for transfers between devices  130 us (61%)
  local copies, waits for them, and re-layouts  21.5 us (10%)
  matrix products  21.1 us (10%)
  between operations  16.5 us (8%)
  starting transfers between devices  12.7 us (6%)
  other arithmetic  10.5 us (5%)
    psum x1, waiting for transfers between devices, shards(): lax.psum((query_grad, out_grad, pair_weight), ('inst', 'lon'))  127 us
    ppermute x1, starting transfers between devices, with_halo(): lax.ppermute(lax.slice_in_dim(block, 0, width, axis=dim), axis, backward)  6.97 us
    unnamed x53, local copies, waits for them, and re-layouts  6.93 us
    ppermute x2, starting transfers between devices, passed_along(): return lax.ppermute(block, axis, route)  5.67 us
  transfers between devices with their start and end apart: 6, of which 3 were waited for; matrix products, arithmetic and copies ran while one was open for 9% of the time, Pallas kernels for 0%

profile of v1, /device:TPU:0, one launch (start us, length us, event | category | flops | bytes accessed | tf_op | source)
XLA Modules:
  0.0 212.4 jit_solution(12087746813177318972)
XLA Ops:
  10.9 7.0 %collective-permute-start.1 = (bf16[2,184,256]{2,1,0:T(8,128)(2,1)}, bf16[2,184,256]{2,1,0:T(8,128)(2,1)}, u32[]{:S(2)}, u32[]{:S(2)}) collective-permute-start(bf16[2,184,256]{2,1,0:T(8,128)(2,1)} %bitcast.7), channel_id=1, source_target_pairs={{1,0},{2,1},{3,2},{4,3},{5,4},{6,5},{7,6},{8,7},{9,8},{10,9},{11,1... | collective-permute-start | bytes 565256 | tf_op jit(solution)/shard_map/ppermute | solution.py:21
  20.1 1.1 reshape.270
  21.9 1.4 broadcast_multiply_fusion
  23.3 1.1 convolution_convert_fusion
  24.4 1.2 copy.37
  25.6 1.1 reshape.275
  28.0 1.1 pad_maximum_fusion
  29.1 2.0 gather_fusion
  32.6 1.2 fusion.36
  35.2 1.1 convolution_convert_fusion.3
  36.3 3.3 %fusion.8 = bf16[12,128,4,32]{1,3,2,0:T(8,128)(2,1)} fusion(bf16[12,25,4,32]{1,3,2,0:T(8,128)(2,1)S(1)} %bitcast.120, f32[12,4,128,25]{2,3,1,0:T(8,128)} %fusion.36, f32[12,4,128,25]{2,3,1,0:T(8,128)} %copy-done.23, f32[12,4,128]{2,1,0:T(4,128)S(1)} %get-tuple-element.62), kind=kOutput, calls=%fused_computation.21 | convolution fusion | flops 11876376 | bytes 1723392 | tf_op jit(solution)/shard_map/nhqk,nkhd->nqhd/dot_general | solution.py:86
  39.5 2.7 %convolution_bitcast_fusion.1 = f32[12,25,4,32]{1,3,2,0:T(8,128)S(1)} fusion(f32[12,4,128,25]{2,3,1,0:T(8,128)} %fusion.36, f32[12,4,128,25]{2,3,1,0:T(8,128)} %copy-done.23, bf16[12,128,4,32]{1,0,3,2:T(8,128)(2,1)} %reshape.270, f32[12,4,128]{2,1,0:T(4,128)S(1)} %get-tuple-element.62), kind=kOutput, calls=%fused_computation.12 | convolution fusion | flops 11679768 | bytes 1800192 | tf_op jit(solution)/shard_map/nhqk,nqhd->nkhd/dot_general | solution.py:90
  42.3 2.4 %convolution_bitcast_fusion = f32[12,25,4,32]{1,3,2,0:T(8,128)} fusion(bf16[12,128,4,32]{1,0,3,2:T(8,128)(2,1)S(1)} %copy-done.6, f32[12,4,128,25]{2,3,1,0:T(8,128)} %copy-done.23, f32[12,4,128]{2,1,0:T(4,128)S(1)} %get-tuple-element.62), kind=kOutput, calls=%fused_computation.11 | convolution fusion | flops 10291200 | bytes 1185792 | tf_op jit(solution)/shard_map/nhqk,nqhd->nkhd/dot_general | solution.py:93
  44.6 1.5 copy.45
  48.4 3.0 %scatter_custom_fusion = f32[1472,256]{1,0:T(8,128)S(1)} fusion(s32[300]{0:T(512)} %fusion.45, f32[]{:T(128)} %constant.106.clone.1, f32[300,128]{1,0:T(8,128)} %concatenate.21, f32[]{:T(128)} %constant.116, f32[300,128]{1,0:T(8,128)} %concatenate.20), kind=kCustom, calls=%fused_computation.37 | custom fusion | flops 153600 | bytes 1819648 | tf_op jit(solution)/shard_map/scatter-add | solution.py:136
  51.5 1.0 copy-done.1
  54.3 5.6 %collective-permute-start.3 = (bf16[2,184,256]{2,1,0:T(8,128)(2,1)S(1)}, bf16[2,184,256]{2,1,0:T(8,128)(2,1)S(1)}, u32[]{:S(2)}, u32[]{:S(2)}) collective-permute-start(bf16[2,184,256]{2,1,0:T(8,128)(2,1)S(1)} %bitcast.121), channel_id=1, source_target_pairs={{1,0},{2,1},{3,2},{4,3},{5,4},{6,5},{7,6},{8,7},{9,8},{10,9},{11,1... | collective-permute-start | bytes 565256 | tf_op jit(solution)/shard_map/ppermute | solution.py:29
  60.8 2.6 %collective-permute-done.2 = bf16[2,184,256]{2,1,0:T(8,128)(2,1)S(1)} collective-permute-done((bf16[2,184,256]{2,1,0:T(8,128)(2,1)S(1)}, bf16[2,184,256]{2,1,0:T(8,128)(2,1)S(1)}, u32[]{:S(2)}, u32[]{:S(2)}) %collective-permute-start.2) | collective-permute-done | bytes 188448 | tf_op jit(solution)/shard_map/ppermute | solution.py:29
  66.1 2.2 %convolution_add_fusion.1 = f32[736,256]{1,0:T(8,128)} fusion(f32[736,256]{1,0:T(8,128)S(1)} %fusion.65, bf16[736,256]{1,0:T(8,128)(2,1)} %get-tuple-element.48, bf16[256,256]{1,0:T(8,128)(2,1)S(1)} %copy-done.8), kind=kOutput, calls=%fused_computation.16 | convolution fusion | flops 96657408 | bytes 2015232 | tf_op jit(solution)/shard_map/dot_general | solution.py:39
  68.4 1.3 fusion.1
  69.7 1.3 add_convert_fusion
  71.1 126.6 %all-reduce.3.cloned.1.call-done = (f32[256,128]{0,1:T(8,128)}, f32[256,256]{0,1:T(8,128)}, f32[128,256]{1,0:T(8,128)}) async-done(((f32[256,128]{0,1:T(8,128)}, f32[256,256]{0,1:T(8,128)}, f32[128,256]{1,0:T(8,128)}), (f32[256,128]{0,1:T(8,128)}, f32[256,256]{0,1:T(8,128)}, f32[128,256]{1,0:T(8,128)})) %all-reduce.3.cloned.1.call-update) | async-done | bytes 524304 | tf_op jit(solution)/shard_map/psum | solution.py:150
  197.7 1.7 copy.47
  201.9 2.4 %reduce_sum.29 = f32[736,256]{1,0:T(8,128)} reduce(f32[2,736,256]{2,1,0:T(8,128)} %bitcast.116, f32[]{:T(128)} %constant.106.clone.1), dimensions={0}, to_apply=%region_3.4 | reduce | flops 188416 | bytes 2260996 | tf_op jit(solution)/shard_map/reduce_sum | solution.py:149
  (109 shorter events, 20.0 us)
Async XLA Ops:
  8.0 1.9 copy-start
  8.0 9.9 %copy-start.22 = (s32[12,2]{0,1:T(2,128)S(1)}, s32[12,2]{0,1:T(2,128)}, u32[]{:S(2)}) copy-start(s32[12,2]{0,1:T(2,128)} %param.16) | copy-start | bytes 292
  8.0 11.5 %copy-start.15 = (bf16[256,128]{1,0:T(8,128)(2,1)S(1)}, bf16[256,128]{1,0:T(8,128)(2,1)}, u32[]{:S(2)}) copy-start(bf16[256,128]{1,0:T(8,128)(2,1)} %param.20) | copy-start | bytes 196612
  8.0 11.5 %copy-start.2 = (bf16[12,128,256]{2,1,0:T(8,128)(2,1)S(1)}, bf16[12,128,256]{2,1,0:T(8,128)(2,1)}, u32[]{:S(2)}) copy-start(bf16[12,128,256]{2,1,0:T(8,128)(2,1)} %param.14) | copy-start | bytes 2359300
  8.0 189.6 %all-reduce.3.cloned.1.call-start = ((), (), s32[]{:S(2)}) async-start(), calls=%async_computation.1 | async-start | bytes 1048576 | tf_op jit(solution)/shard_map/psum | solution.py:150
  9.9 10.0 %copy-start.7 = (bf16[256,256]{1,0:T(8,128)(2,1)}, bf16[256,256]{1,0:T(8,128)(2,1)S(1)}, u32[]{:S(2)}) copy-start(bf16[256,256]{1,0:T(8,128)(2,1)S(1)} %constant_dynamic-update-slice_fusion) | copy-start | bytes 393220
  10.9 16.3 %collective-permute-start.1 = (bf16[2,184,256]{2,1,0:T(8,128)(2,1)}, bf16[2,184,256]{2,1,0:T(8,128)(2,1)}, u32[]{:S(2)}, u32[]{:S(2)}) collective-permute-start(bf16[2,184,256]{2,1,0:T(8,128)(2,1)} %bitcast.7), channel_id=1, source_target_pairs={{1,0},{2,1},{3,2},{4,3},{5,4},{6,5},{7,6},{8,7},{9,8},{10,9},{11,1... | collective-permute-start | bytes 565256 | tf_op jit(solution)/shard_map/ppermute | solution.py:21
  17.9 10.1 %collective-permute-start = (bf16[2,184,256]{2,1,0:T(8,128)(2,1)}, bf16[2,184,256]{2,1,0:T(8,128)(2,1)}, u32[]{:S(2)}, u32[]{:S(2)}) collective-permute-start(bf16[2,184,256]{2,1,0:T(8,128)(2,1)} %bitcast.5), channel_id=1, source_target_pairs={{0,1},{1,2},{2,3},{3,4},{4,5},{5,6},{6,7},{7,8},{8,9},{9,10},{10,1... | collective-permute-start | bytes 565256 | tf_op jit(solution)/shard_map/ppermute | solution.py:18
  19.4 1.9 copy-start.21
  19.9 3.4 %copy-start.17 = (bf16[128,256]{1,0:T(8,128)(2,1)S(1)}, bf16[128,256]{1,0:T(8,128)(2,1)}, u32[]{:S(2)}) copy-start(bf16[128,256]{1,0:T(8,128)(2,1)} %param.23) | copy-start | bytes 196612
  31.1 1.5 copy-start.6
  31.3 2.5 %copy-start.11 = (bf16[12,128,4,32]{1,0,3,2:T(8,128)(2,1)S(1)}, bf16[12,128,4,32]{1,0,3,2:T(8,128)(2,1)}, u32[]{:S(2)}) copy-start(bf16[12,128,4,32]{1,0,3,2:T(8,128)(2,1)} %reshape.270) | copy-start | bytes 1179652
  51.5 2.4 %copy-start.9 = (bf16[12,4,32,128]{3,2,1,0:T(8,128)(2,1)S(1)}, bf16[12,4,32,128]{3,2,1,0:T(8,128)(2,1)}, u32[]{:S(2)}) copy-start(bf16[12,4,32,128]{3,2,1,0:T(8,128)(2,1)} %convolution_convert_fusion.3) | copy-start | bytes 1179652
  53.0 7.9 %copy-start.3 = (bf16[12,128,4,32]{1,0,3,2:T(8,128)(2,1)}, bf16[12,128,4,32]{1,0,3,2:T(8,128)(2,1)S(1)}, u32[]{:S(2)}) copy-start(bf16[12,128,4,32]{1,0,3,2:T(8,128)(2,1)S(1)} %copy.41) | copy-start | bytes 1179652
  53.9 9.6 %slice-start = ((f32[1472,256]{1,0:T(8,128)}), f32[368,256]{1,0:T(8,128)S(1)}, s32[]{:S(2)}) async-start(f32[1472,256]{1,0:T(8,128)} %copy-done.1), calls=%async_computation.2 | async-start | bytes 753664 | tf_op jit(solution)/shard_map/slice.60
  53.9 9.6 %slice-start.1 = ((f32[1472,256]{1,0:T(8,128)}), f32[736,256]{1,0:T(8,128)S(1)}, s32[]{:S(2)}) async-start(f32[1472,256]{1,0:T(8,128)} %copy-done.1), calls=%async_computation.3 | async-start | bytes 1507328 | tf_op jit(solution)/shard_map/slice | solution.py:142
  54.2 9.2 %collective-permute-start.2 = (bf16[2,184,256]{2,1,0:T(8,128)(2,1)S(1)}, bf16[2,184,256]{2,1,0:T(8,128)(2,1)S(1)}, u32[]{:S(2)}, u32[]{:S(2)}) collective-permute-start(bf16[2,184,256]{2,1,0:T(8,128)(2,1)S(1)} %bitcast.122), channel_id=1, source_target_pairs={{15,0},{0,1},{1,2},{2,3},{3,4},{4,5},{5,6},{6,7},{7,8},{8,9},{9,10... | collective-permute-start | bytes 565256 | tf_op jit(solution)/shard_map/ppermute | solution.py:29
  54.3 9.2 %collective-permute-start.3 = (bf16[2,184,256]{2,1,0:T(8,128)(2,1)S(1)}, bf16[2,184,256]{2,1,0:T(8,128)(2,1)S(1)}, u32[]{:S(2)}, u32[]{:S(2)}) collective-permute-start(bf16[2,184,256]{2,1,0:T(8,128)(2,1)S(1)} %bitcast.121), channel_id=1, source_target_pairs={{1,0},{2,1},{3,2},{4,3},{5,4},{6,5},{7,6},{8,7},{9,8},{10,9},{11,1... | collective-permute-start | bytes 565256 | tf_op jit(solution)/shard_map/ppermute | solution.py:29
  63.9 1.8 copy-start.8
  66.1 2.4 %copy-start.4 = (bf16[12,128,4,32]{1,0,3,2:T(8,128)(2,1)S(1)}, bf16[12,128,4,32]{1,0,3,2:T(8,128)(2,1)}, u32[]{:S(2)}) copy-start(bf16[12,128,4,32]{1,0,3,2:T(8,128)(2,1)} %copy-done.3) | copy-start | bytes 1179652
  66.1 2.4 %copy-start.5 = (bf16[12,128,256]{2,1,0:T(8,128)(2,1)S(1)}, bf16[12,128,256]{2,1,0:T(8,128)(2,1)}, u32[]{:S(2)}) copy-start(bf16[12,128,256]{2,1,0:T(8,128)(2,1)} %param.15) | copy-start | bytes 2359300
  66.1 2.4 %copy-start.16 = (bf16[256,128]{1,0:T(8,128)(2,1)S(1)}, bf16[256,128]{1,0:T(8,128)(2,1)}, u32[]{:S(2)}) copy-start(bf16[256,128]{1,0:T(8,128)(2,1)} %param.20) | copy-start | bytes 196612
  66.1 135.8 %all-gather.3.cloned.1.call-start = ((), (), s32[]{:S(2)}) async-start(), calls=%async_computation | async-start | bytes 2260992 | tf_op jit(solution)/shard_map/all_gather | solution.py:148
  200.3 4.0 %copy-start.19 = (f32[128,256]{1,0:T(8,128)S(1)}, f32[128,256]{1,0:T(8,128)}, u32[]{:S(2)}) copy-start(f32[128,256]{1,0:T(8,128)} %get-tuple-element.72) | copy-start | bytes 393220
  (8 other events, 9.6 us)
Sparse Core Ops, SparseCore 0:
  66.2 131.4 all-reduce.2
Sparse Core Ops, SparseCore 1:
  68.7 10.9 all-gather.2
